TPU v7x, 128 devices: a whole 4x4x4 slice. The times are simulated.
128 devices in a mesh: row: 8 (over y, z_lo), col: 16 (over x, z_hi, core).
Axes of the slice: x: 4, y: 4, z: 4 (z_hi: 2, z_lo: 2; z = z_hi * 2 + z_lo), core: 2. Of those that a mesh axis runs over, the one named last changes fastest.
Arguments:
- tokens: bfloat16 [1024, 53248], P(('row', 'col')), may hold values from -6 to 6
- eigvecs: float32 [53248, 2048], P('row', 'col'), may hold values from -0.02734375 to 0.02734375
- eigvals: float32 [2048], P('col'), may hold values from 0.25 to 4
- v_first: float32 [53248, 256], P(('row', 'col')), may hold values from -0.109375 to 0.109375
- v_second: float32 [53248, 256], P(('row', 'col')), may hold values from -0.109375 to 0.109375
- t_first: float32 [256, 256], replicated, may hold values from -0.375 to 0.375
- t_second: float32 [256, 256], replicated, may hold values from -0.375 to 0.375
Outputs:
- whitened: float32 [1024, 2048], P('row', 'col')
All inputs are finite; a program needn't handle non-finite values.
Results may differ from a plain program's by a relative error of at most 0.0029.
Values may be sent and summed in bfloat16 or wider, within the bound.
A program may use at most 128 MiB of HBM per device.

v0:
```python
import jax
import jax.numpy as jnp
from jax import lax
from jax.sharding import PartitionSpec as P


def local_update(block, panel, factor, inner):
    middle = jnp.dot(
        factor, inner, precision=lax.Precision.HIGHEST, preferred_element_type=jnp.float32
    )
    return block - jnp.dot(
        panel, middle, precision=lax.Precision.HIGHEST, preferred_element_type=jnp.float32
    )


def partial_inner(panel, block):
    return jnp.dot(
        panel.T, block, precision=lax.Precision.HIGHEST, preferred_element_type=jnp.float32
    )


def per_device(tokens, eigvecs, eigvals, v_first, v_second, t_first, t_second):
    panels = (
        lax.all_gather(v_first, "col", axis=0, tiled=True),
        lax.all_gather(v_second, "col", axis=0, tiled=True),
    )
    block = eigvecs
    for panel, factor in ((panels[1], t_second), (panels[0], t_first)):
        inner = lax.psum(partial_inner(panel, block), "row")
        block = local_update(block, panel, factor, inner)
    whitening = (block * lax.rsqrt(eigvals)[None, :]).astype(jnp.bfloat16)
    row_tokens = lax.all_gather(tokens, "col", axis=0, tiled=True)
    slab = lax.all_to_all(row_tokens, "row", split_axis=1, concat_axis=0, tiled=True)
    partial_value = jnp.dot(slab, whitening, preferred_element_type=jnp.float32)
    summed = lax.psum_scatter(partial_value, "row", scatter_dimension=0, tiled=True)
    return summed


def solution(mesh):
    in_specs = (
        P(("row", "col"), None),
        P("row", "col"),
        P("col"),
        P(("row", "col"), None),
        P(("row", "col"), None),
        P(),
        P(),
    )
    out_specs = P("row", "col")
    return jax.shard_map(
        per_device, mesh=mesh, in_specs=in_specs, out_specs=out_specs, check_vma=False
    )
```

profile of v0, /device:TPU:0, one launch (start us, length us, event | category | flops | bytes accessed | tf_op | source)
XLA Modules:
  0.0 653.4 jit_solution(17153606568712980208)
XLA Ops:
  6.5 0.0 copy-start
  6.5 0.0 all-gather.4.cloned.1.call-start
  6.5 0.7 all-gather.4.cloned.1.call-update
  7.3 0.0 all-gather.8.cloned.1.call-start
  7.3 0.7 all-gather.8.cloned.1.call-update
  8.0 0.0 all-reduce.3.cloned.1.call-start
  8.1 70.6 %all-gather.4.cloned.1.call-done = f32[6656,256]{1,0:T(8,128)} async-done(((f32[416,256]{1,0:T(8,128)}), f32[6656,256]{1,0:T(8,128)}) %all-gather.4.cloned.1.call-update) | async-done | bytes 6815760 | tf_op jit(solution)/shard_map/all_gather | solution.py:25
  78.7 14.6 %fusion.4 = f32[256,128]{1,0:T(8,128)} fusion(f32[6656,256]{1,0:T(8,128)} %all-gather.4.cloned.1.call-done, f32[6656,128]{1,0:T(8,128)} %param.8), kind=kOutput, calls=%fused_computation.8 | convolution fusion | flops 2617245696 | bytes 10354688 | tf_op jit(solution)/shard_map/dot_general | solution.py:17
  93.3 0.0 all-reduce.3.cloned.1.call-update
  93.4 0.0 all-gather.6.cloned.1.call-start
  93.4 0.5 all-gather.6.cloned.1.call-update
  94.0 80.9 %all-gather.8.cloned.1.call-done = bf16[128,53248]{1,0:T(8,128)(2,1)} async-done(((bf16[8,53248]{1,0:T(8,128)(2,1)}), bf16[128,53248]{1,0:T(8,128)(2,1)}) %all-gather.8.cloned.1.call-update) | async-done | bytes 13631504 | tf_op jit(solution)/shard_map/all_gather | solution.py:32
  174.8 18.4 %copy.17 = bf16[128,53248]{0,1:T(8,128)(2,1)} copy(bf16[128,53248]{1,0:T(8,128)(2,1)} %all-gather.8.cloned.1.call-done) | data formatting | bytes 27262976 | tf_op jit(solution)/shard_map/all_gather | solution.py:32
  193.2 5.4 all-to-all-start
  198.7 0.2 all-reduce.5.cloned.1.call-start
  198.9 5.1 copy.16
  204.0 216.3 %all-reduce.3.cloned.1.call-done = f32[256,128]{1,0:T(8,128)} async-done(((f32[256,128]{1,0:T(8,128)}), f32[256,128]{1,0:T(8,128)}) %all-reduce.3.cloned.1.call-update) | async-done | bytes 131088 | tf_op jit(solution)/shard_map/psum | solution.py:29
  420.3 0.0 copy-done
  420.3 1.3 fusion.5
  421.6 12.6 %fusion.2 = f32[6656,128]{0,1:T(8,128)} fusion(f32[6656,128]{0,1:T(8,128)} %copy.16, f32[128,256]{1,0:T(8,128)S(1)} %fusion.5, f32[6656,256]{1,0:T(8,128)} %all-gather.4.cloned.1.call-done), kind=kOutput, calls=%fused_computation.4 | convolution fusion | flops 2618097664 | bytes 13762560 | tf_op jit(solution)/shard_map/dot_general | solution.py:11
  434.2 0.0 copy-start.3
  434.2 0.0 copy-start.2
  434.2 54.4 %all-gather.6.cloned.1.call-done = f32[6656,256]{1,0:T(8,128)} async-done(((f32[416,256]{1,0:T(8,128)}), f32[6656,256]{1,0:T(8,128)}) %all-gather.6.cloned.1.call-update) | async-done | bytes 6815760 | tf_op jit(solution)/shard_map/all_gather | solution.py:24
  488.6 7.9 %convolution_bitcast_fusion.3 = f32[256,128]{0,1:T(8,128)} fusion(f32[6656,128]{0,1:T(8,128)} %fusion.2, f32[6656,256]{1,0:T(8,128)} %all-gather.6.cloned.1.call-done), kind=kOutput, calls=%fused_computation.7 | convolution fusion | flops 2617245696 | bytes 10354688 | tf_op jit(solution)/shard_map/dot_general | solution.py:17
  496.5 0.0 all-reduce.5.cloned.1.call-update
  496.5 0.3 reduce-scatter.2.cloned.1.call-start
  496.8 0.0 copy-done.3
  496.8 71.0 %all-reduce.5.cloned.1.call-done = f32[256,128]{0,1:T(8,128)} async-done(((f32[256,128]{0,1:T(8,128)}), f32[256,128]{0,1:T(8,128)}) %all-reduce.5.cloned.1.call-update) | async-done | bytes 131088 | tf_op jit(solution)/shard_map/psum | solution.py:29
  567.8 0.0 copy-done.2
  567.8 1.3 fusion.6
  569.1 10.8 %fusion.3 = bf16[6656,128]{0,1:T(8,128)(2,1)S(1)} fusion(f32[6656,128]{0,1:T(8,128)} %fusion.2, f32[128,256]{1,0:T(8,128)S(1)} %fusion.6, f32[6656,256]{1,0:T(8,128)} %all-gather.6.cloned.1.call-done, f32[128]{0:T(128)S(1)} %rsqrt.3), kind=kOutput, calls=%fused_computation.5 | convolution fusion | flops 2619801600 | bytes 12059136 | tf_op jit(solution)/shard_map/dot_general | solution.py:11
  579.9 0.0 all-to-all-done
  579.9 17.6 %copy.18 = bf16[8,128,6656]{2,1,0:T(8,128)(2,1)} copy(bf16[8,128,6656]{1,2,0:T(8,128)(2,1)} %bitcast.4) | data formatting | bytes 27262976 | tf_op jit(solution)/shard_map/all_to_all | solution.py:33
  597.5 0.0 copy-start.1
  597.5 10.1 %convolution_bitcast_fusion.2 = f32[1024,128]{0,1:T(8,128)} fusion(bf16[6656,128]{0,1:T(8,128)(2,1)S(1)} %fusion.3, bf16[1024,6656]{1,0:T(8,128)(2,1)} %bitcast.34), kind=kOutput, calls=%fused_computation.6 | convolution fusion | flops 1744830464 | bytes 15859712 | tf_op jit(solution)/shard_map/dot_general | solution.py:34
  607.6 0.0 reduce-scatter.2.cloned.1.call-update
  607.6 37.4 %reduce-scatter.2.cloned.1.call-done = f32[128,128]{0,1:T(8,128)} async-done(((f32[1024,128]{0,1:T(8,128)}), f32[128,128]{0,1:T(8,128)}) %reduce-scatter.2.cloned.1.call-update) | async-done | bytes 65552 | tf_op jit(solution)/shard_map/reduce_scatter | solution.py:35
  645.0 1.6 copy.19
  646.6 0.0 copy-done.1
  (1 shorter events, 0.0 us)
Async XLA Ops:
  6.5 413.8 %copy-start = (f32[256,256]{1,0:T(8,128)S(1)}, f32[256,256]{1,0:T(8,128)}, u32[]{:S(2)}) copy-start(f32[256,256]{1,0:T(8,128)} %param.13) | copy-start | bytes 786436
  6.5 72.2 %all-gather.4.cloned.1.call-start = ((), (), s32[]{:S(2)}) async-start(), calls=%async_computation.2 | async-start | bytes 7241728 | tf_op jit(solution)/shard_map/all_gather | solution.py:25
  7.3 167.6 %all-gather.8.cloned.1.call-start = ((), (), s32[]{:S(2)}) async-start(), calls=%async_computation.6 | async-start | bytes 14483456 | tf_op jit(solution)/shard_map/all_gather | solution.py:32
  8.0 412.3 %all-reduce.3.cloned.1.call-start = ((), (), s32[]{:S(2)}) async-start(), calls=%async_computation.3 | async-start | bytes 262144 | tf_op jit(solution)/shard_map/psum | solution.py:29
  93.4 395.2 %all-gather.6.cloned.1.call-start = ((), (), s32[]{:S(2)}) async-start(), calls=%async_computation.4 | async-start | bytes 7241728 | tf_op jit(solution)/shard_map/all_gather | solution.py:24
  193.2 386.7 %all-to-all-start = ((bf16[128,8,6656]{0,2,1:T(8,128)(2,1)}), bf16[128,8,6656]{0,2,1:T(8,128)(2,1)}, u32[]{:S(2)}, u32[]{:S(2)}) async-start(bf16[128,8,6656]{0,2,1:T(8,128)(2,1)} %bitcast.33), calls=%async_computation | async-start | bytes 27262976 | tf_op jit(solution)/shard_map/all_to_all | solution.py:33
  198.7 369.1 %all-reduce.5.cloned.1.call-start = ((), (), s32[]{:S(2)}) async-start(), calls=%async_computation.5 | async-start | bytes 262144 | tf_op jit(solution)/shard_map/psum | solution.py:29
  434.2 62.6 %copy-start.3 = (f32[128]{0:T(128)S(1)}, f32[128]{0:T(128)}, u32[]{:S(2)}) copy-start(f32[128]{0:T(128)} %param.9) | copy-start | bytes 1540
  434.2 133.6 %copy-start.2 = (f32[256,256]{1,0:T(8,128)S(1)}, f32[256,256]{1,0:T(8,128)}, u32[]{:S(2)}) copy-start(f32[256,256]{1,0:T(8,128)} %param.12) | copy-start | bytes 786436
  496.5 148.5 %reduce-scatter.2.cloned.1.call-start = ((), (), s32[]{:S(2)}) async-start(), calls=%async_computation.7 | async-start | bytes 589824 | tf_op jit(solution)/shard_map/reduce_scatter | solution.py:35
  597.5 49.1 %copy-start.1 = (f32[256,256]{1,0:T(8,128)S(1)}, f32[256,256]{1,0:T(8,128)}, u32[]{:S(2)}) copy-start(f32[256,256]{1,0:T(8,128)} %param.13) | copy-start | bytes 786436
Sparse Core Ops, SparseCore 0:
  9.8 68.8 all-gather.3
  81.1 93.6 all-gather.7
  177.3 242.9 all-reduce.2
  422.8 65.6 all-gather.5
  496.6 71.0 all-reduce.4
  607.7 37.2 reduce-scatter.1
where the time goes:
time: 655 us; the launch traced here: 653 us
  waiting for transfers between devices  533 us (81%)
  matrix products  58.7 us (9%)
  local copies, waits for them, and re-layouts  42.6 us (7%)
  between operations  13.5 us (2%)
    psum x2, waiting for transfers between devices, per_device(): inner = lax.psum(partial_inner(panel, block), 'row')  287 us
    all_gather x1, waiting for transfers between devices, per_device(): row_tokens = lax.all_gather(tokens, 'col', axis=0, tiled=True)  80.9 us
    all_gather x1, waiting for transfers between devices, per_device(): lax.all_gather(v_second, 'col', axis=0, tiled=True)  70.6 us
    all_gather x1, waiting for transfers between devices, per_device(): lax.all_gather(v_first, 'col', axis=0, tiled=True)  54.4 us
    reduce_scatter x1, waiting for transfers between devices, per_device(): lax.psum_scatter(partial_value, 'row', scatter_dimension=0, tiled=True)  37.4 us
    dot_general x2, matrix products, local_update(): jnp.dot(panel, middle, precision=lax.Precision.HIGHEST, preferred_element...  23.4 us
    dot_general x2, matrix products, partial_inner(): jnp.dot(panel.T, block, precision=lax.Precision.HIGHEST, preferred_elemen...  22.6 us
    all_gather x1, local copies, waits for them, and re-layouts, per_device(): row_tokens = lax.all_gather(tokens, 'col', axis=0, tiled=True)  18.4 us
  transfers between devices with their start and end apart: 7, of which 6 were waited for; matrix products, arithmetic and copies ran while one was open for 11% of the time, Pallas kernels for 0%

commit v1 on v0

--- a/solution.py
+++ b/solution.py
@@ -26,7 +26,9 @@
     )
     block = eigvecs
     for panel, factor in ((panels[1], t_second), (panels[0], t_first)):
-        inner = lax.psum(partial_inner(panel, block), "row")
+        own = partial_inner(panel, block)
+        parts = lax.all_gather(own, "row")
+        inner = jnp.sum(parts, axis=0)
         block = local_update(block, panel, factor, inner)
     whitening = (block * lax.rsqrt(eigvals)[None, :]).astype(jnp.bfloat16)
     row_tokens = lax.all_gather(tokens, "col", axis=0, tiled=True)

time: 655 us -> 589 us (0.90)
  waiting for transfers between devices: 533 us -> 465 us
    psum x2 -> x0, waiting for transfers between devices: 287 us -> none  [per_device(): inner = lax.psum(partial_inner(panel, block), 'row')]
    all_gather x0 -> x2, waiting for transfers between devices: none -> 188 us  [per_device(): parts = lax.all_gather(own, 'row')]
    all_gather x1, waiting for transfers between devices: 54.4 us -> 85.4 us  [per_device(): lax.all_gather(v_first, 'col', axis=0, tiled=True)]
  transfers between devices with their start and end apart: 7 -> 7, of which waited for: 6 -> 6; matrix products, arithmetic and copies ran while one was open for 11% -> 12% of each run, Pallas kernels for 0% -> 0%
where the time goes in v1:
time: 589 us; the launch traced here: 587 us
  waiting for transfers between devices  465 us (79%)
  matrix products  56.9 us (10%)
  local copies, waits for them, and re-layouts  44.2 us (8%)
  between operations  13.6 us (2%)
  starting transfers between devices  6.05 us (1%)
    all_gather x2, waiting for transfers between devices, per_device(): parts = lax.all_gather(own, 'row')  188 us
    all_gather x1, waiting for transfers between devices, per_device(): lax.all_gather(v_first, 'col', axis=0, tiled=True)  85.4 us
    all_gather x1, waiting for transfers between devices, per_device(): row_tokens = lax.all_gather(tokens, 'col', axis=0, tiled=True)  80.9 us
    all_gather x1, waiting for transfers between devices, per_device(): lax.all_gather(v_second, 'col', axis=0, tiled=True)  70.6 us
    reduce_scatter x1, waiting for transfers between devices, per_device(): lax.psum_scatter(partial_value, 'row', scatter_dimension=0, tiled=True)  37.8 us
    dot_general x2, matrix products, local_update(): jnp.dot(panel, middle, precision=lax.Precision.HIGHEST, preferred_element...  23.4 us
    dot_general x2, matrix products, partial_inner(): jnp.dot(panel.T, block, precision=lax.Precision.HIGHEST, preferred_elemen...  22.5 us
    all_gather x1, local copies, waits for them, and re-layouts, per_device(): row_tokens = lax.all_gather(tokens, 'col', axis=0, tiled=True)  18.4 us
  transfers between devices with their start and end apart: 7, of which 6 were waited for; matrix products, arithmetic and copies ran while one was open for 12% of the time, Pallas kernels for 0%

profile of v1, /device:TPU:0, one launch (start us, length us, event | category | flops | bytes accessed | tf_op | source)
XLA Modules:
  0.0 587.3 jit_solution(6696955592179137621)
XLA Ops:
  6.5 0.0 copy-start
  6.5 0.0 all-gather.8.cloned.1.call-start
  6.5 0.7 all-gather.8.cloned.1.call-update
  7.3 0.0 all-gather.12.cloned.1.call-start
  7.3 0.7 all-gather.12.cloned.1.call-update
  8.0 0.0 all-gather.14.cloned.1.call-start
  8.1 70.6 %all-gather.8.cloned.1.call-done = f32[6656,256]{1,0:T(8,128)} async-done(((f32[416,256]{1,0:T(8,128)}), f32[6656,256]{1,0:T(8,128)}) %all-gather.8.cloned.1.call-update) | async-done | bytes 6815760 | tf_op jit(solution)/shard_map/all_gather | solution.py:25
  78.7 14.6 %fusion.4 = f32[256,128]{1,0:T(8,128)} fusion(f32[6656,256]{1,0:T(8,128)} %all-gather.8.cloned.1.call-done, f32[6656,128]{1,0:T(8,128)} %param.8), kind=kOutput, calls=%fused_computation.9 | convolution fusion | flops 2617245696 | bytes 10354688 | tf_op jit(solution)/shard_map/dot_general | solution.py:17
  93.3 0.0 all-gather.14.cloned.1.call-update
  93.3 0.0 all-gather.10.cloned.1.call-start
  93.4 0.5 all-gather.10.cloned.1.call-update
  93.9 80.9 %all-gather.12.cloned.1.call-done = bf16[128,53248]{1,0:T(8,128)(2,1)} async-done(((bf16[8,53248]{1,0:T(8,128)(2,1)}), bf16[128,53248]{1,0:T(8,128)(2,1)}) %all-gather.12.cloned.1.call-update) | async-done | bytes 13631504 | tf_op jit(solution)/shard_map/all_gather | solution.py:34
  174.8 18.4 %copy.17 = bf16[128,53248]{0,1:T(8,128)(2,1)} copy(bf16[128,53248]{1,0:T(8,128)(2,1)} %all-gather.12.cloned.1.call-done) | data formatting | bytes 27262976 | tf_op jit(solution)/shard_map/all_gather | solution.py:34
  193.2 5.4 all-to-all-start
  198.7 0.2 all-gather.16.cloned.1.call-start
  198.9 5.1 copy.16
  204.0 151.5 %all-gather.14.cloned.1.call-done = f32[2048,128]{1,0:T(8,128)} async-done(((f32[256,128]{1,0:T(8,128)}), f32[2048,128]{1,0:T(8,128)}) %all-gather.14.cloned.1.call-update) | async-done | bytes 1048592 | tf_op jit(solution)/shard_map/all_gather | solution.py:30
  355.5 1.3 reduce_sum.18
  356.8 0.0 copy-done
  356.8 0.4 fusion.5
  357.2 12.6 %fusion.2 = f32[6656,128]{0,1:T(8,128)} fusion(f32[6656,128]{0,1:T(8,128)} %copy.16, f32[128,256]{1,0:T(8,128)S(1)} %fusion.5, f32[6656,256]{1,0:T(8,128)} %all-gather.8.cloned.1.call-done), kind=kOutput, calls=%fused_computation.4 | convolution fusion | flops 2618097664 | bytes 13762560 | tf_op jit(solution)/shard_map/dot_general | solution.py:11
  369.8 0.0 copy-start.3
  369.8 85.4 %all-gather.10.cloned.1.call-done = f32[6656,256]{1,0:T(8,128)} async-done(((f32[416,256]{1,0:T(8,128)}), f32[6656,256]{1,0:T(8,128)}) %all-gather.10.cloned.1.call-update) | async-done | bytes 6815760 | tf_op jit(solution)/shard_map/all_gather | solution.py:24
  455.2 7.9 %convolution_bitcast_fusion.3 = f32[256,128]{0,1:T(8,128)} fusion(f32[6656,128]{0,1:T(8,128)} %fusion.2, f32[6656,256]{1,0:T(8,128)} %all-gather.10.cloned.1.call-done), kind=kOutput, calls=%fused_computation.7 | convolution fusion | flops 2617245696 | bytes 10354688 | tf_op jit(solution)/shard_map/dot_general | solution.py:17
  463.1 0.0 copy-start.2
  463.1 0.0 all-gather.16.cloned.1.call-update
  463.1 0.3 reduce-scatter.2.cloned.1.call-start
  463.4 0.0 copy-done.3
  463.4 36.8 %all-gather.16.cloned.1.call-done = f32[2048,128]{0,1:T(8,128)} async-done(((f32[256,128]{0,1:T(8,128)}), f32[2048,128]{0,1:T(8,128)}) %all-gather.16.cloned.1.call-update) | async-done | bytes 1048592 | tf_op jit(solution)/shard_map/all_gather | solution.py:30
  500.2 1.6 copy.20
  501.8 0.3 bitcast_reduce_fusion
  502.1 0.0 copy-done.2
  502.1 0.4 fusion.6
  502.5 10.8 %fusion.3 = bf16[6656,128]{0,1:T(8,128)(2,1)S(1)} fusion(f32[6656,128]{0,1:T(8,128)} %fusion.2, f32[128,256]{1,0:T(8,128)S(1)} %fusion.6, f32[6656,256]{1,0:T(8,128)} %all-gather.10.cloned.1.call-done, f32[128]{0:T(128)S(1)} %rsqrt.3), kind=kOutput, calls=%fused_computation.5 | convolution fusion | flops 2619801600 | bytes 12059136 | tf_op jit(solution)/shard_map/dot_general | solution.py:11
  513.3 0.0 all-to-all-done
  513.3 17.6 %copy.18 = bf16[8,128,6656]{2,1,0:T(8,128)(2,1)} copy(bf16[8,128,6656]{1,2,0:T(8,128)(2,1)} %bitcast.5) | data formatting | bytes 27262976 | tf_op jit(solution)/shard_map/all_to_all | solution.py:35
  530.9 0.0 copy-start.1
  530.9 10.1 %convolution_bitcast_fusion.2 = f32[1024,128]{0,1:T(8,128)} fusion(bf16[6656,128]{0,1:T(8,128)(2,1)S(1)} %fusion.3, bf16[1024,6656]{1,0:T(8,128)(2,1)} %bitcast.40), kind=kOutput, calls=%fused_computation.6 | convolution fusion | flops 1744830464 | bytes 15859712 | tf_op jit(solution)/shard_map/dot_general | solution.py:36
  541.0 0.0 reduce-scatter.2.cloned.1.call-update
  541.0 37.8 %reduce-scatter.2.cloned.1.call-done = f32[128,128]{0,1:T(8,128)} async-done(((f32[1024,128]{0,1:T(8,128)}), f32[128,128]{0,1:T(8,128)}) %reduce-scatter.2.cloned.1.call-update) | async-done | bytes 65552 | tf_op jit(solution)/shard_map/reduce_scatter | solution.py:37
  578.9 1.6 copy.19
  580.4 0.0 copy-done.1
  (1 shorter events, 0.0 us)
Async XLA Ops:
  6.5 350.3 %copy-start = (f32[256,256]{1,0:T(8,128)S(1)}, f32[256,256]{1,0:T(8,128)}, u32[]{:S(2)}) copy-start(f32[256,256]{1,0:T(8,128)} %param.13) | copy-start | bytes 786436
  6.5 72.2 %all-gather.8.cloned.1.call-start = ((), (), s32[]{:S(2)}) async-start(), calls=%async_computation.2 | async-start | bytes 7241728 | tf_op jit(solution)/shard_map/all_gather | solution.py:25
  7.3 167.6 %all-gather.12.cloned.1.call-start = ((), (), s32[]{:S(2)}) async-start(), calls=%async_computation.4 | async-start | bytes 14483456 | tf_op jit(solution)/shard_map/all_gather | solution.py:34
  8.0 347.5 %all-gather.14.cloned.1.call-start = ((), (), s32[]{:S(2)}) async-start(), calls=%async_computation.6 | async-start | bytes 1179648 | tf_op jit(solution)/shard_map/all_gather | solution.py:30
  93.3 361.8 %all-gather.10.cloned.1.call-start = ((), (), s32[]{:S(2)}) async-start(), calls=%async_computation.3 | async-start | bytes 7241728 | tf_op jit(solution)/shard_map/all_gather | solution.py:24
  193.2 320.1 %all-to-all-start = ((bf16[128,8,6656]{0,2,1:T(8,128)(2,1)}), bf16[128,8,6656]{0,2,1:T(8,128)(2,1)}, u32[]{:S(2)}, u32[]{:S(2)}) async-start(bf16[128,8,6656]{0,2,1:T(8,128)(2,1)} %bitcast.39), calls=%async_computation | async-start | bytes 27262976 | tf_op jit(solution)/shard_map/all_to_all | solution.py:35
  198.7 301.6 %all-gather.16.cloned.1.call-start = ((), (), s32[]{:S(2)}) async-start(), calls=%async_computation.7 | async-start | bytes 1179648 | tf_op jit(solution)/shard_map/all_gather | solution.py:30
  369.8 93.6 %copy-start.3 = (f32[128]{0:T(128)S(1)}, f32[128]{0:T(128)}, u32[]{:S(2)}) copy-start(f32[128]{0:T(128)} %param.9) | copy-start | bytes 1540
  463.1 39.0 %copy-start.2 = (f32[256,256]{1,0:T(8,128)S(1)}, f32[256,256]{1,0:T(8,128)}, u32[]{:S(2)}) copy-start(f32[256,256]{1,0:T(8,128)} %param.12) | copy-start | bytes 786436
  463.1 115.7 %reduce-scatter.2.cloned.1.call-start = ((), (), s32[]{:S(2)}) async-start(), calls=%async_computation.5 | async-start | bytes 589824 | tf_op jit(solution)/shard_map/reduce_scatter | solution.py:37
  530.9 49.5 %copy-start.1 = (f32[256,256]{1,0:T(8,128)S(1)}, f32[256,256]{1,0:T(8,128)}, u32[]{:S(2)}) copy-start(f32[256,256]{1,0:T(8,128)} %param.13) | copy-start | bytes 786436
Sparse Core Ops, SparseCore 0:
  9.8 68.8 all-gather.7
  81.1 93.6 all-gather.11
  176.5 179.0 all-gather.13
  357.8 97.3 all-gather.9
  463.3 36.9 all-gather.15
  541.2 37.6 reduce-scatter.1
